TPU v7x, 32 devices: a whole 2x2x4 slice. The times are simulated.
32 devices in a mesh: groups: 2 (over x), seq: 16 (over z, y, core).
Axes of the slice: x: 2, y: 2, z: 4, core: 2. Of those that a mesh axis runs over, the one named last changes fastest.
Arguments:
- tokens: bfloat16 [96, 5120], P(('groups', 'seq')), parts along dimension 0, may hold values from -6 to 6
- modulation: float32 [6, 5120], replicated, may hold values from -2.5 to 2.5
- w_qkv: bfloat16 [3, 5120, 2560], P(None, None, 'seq'), may hold values from -0.078125 to 0.078125
- norm_gains: float32 [2, 2560], replicated, may hold values from 0.56 to 12
- cache_kv: bfloat16 [2, 2, 96, 2560], P(None, None, ('groups', 'seq')), parts along dimension 2, may hold values from -17 to 17
- w_out: bfloat16 [2560, 5120], P(None, 'seq'), may hold values from -0.125 to 0.125
- w_up: bfloat16 [5120, 13824], P(None, 'seq'), may hold values from -0.078125 to 0.078125
- w_down: bfloat16 [13824, 5120], P('seq'), may hold values from -0.0546875 to 0.0546875
Outputs:
- block_out: bfloat16 [96, 5120], P(('groups', 'seq')), parts along dimension 0
There are 2 independent parts, one for each index of `groups`. A program takes and returns all parts, laid end to end along the dimension named above; an argument that names none is the same for every part. Nothing has to cross between parts.
All inputs are finite; a program needn't handle non-finite values.
Results may differ from a plain program's by a relative error of at most 0.017.
The roundings to bfloat16 on the way count: a program that leaves them out, or rounds other values in their place, can miss the bound.
Values may be sent and summed in bfloat16 or wider, within the bound.
A program may use at most 128 MiB of HBM per device.

v0:
```python
import math

import jax
import jax.numpy as jnp
from jax import lax
from jax.sharding import PartitionSpec as P

HEAD_DIM = 128
HEADS = 20


def layer_norm(values):
    center = values - jnp.mean(values, axis=-1, keepdims=True)
    spread = jnp.mean(center * center, axis=-1, keepdims=True)
    return center * lax.rsqrt(spread + 1e-06)


def rms_norm(values, gain):
    return values * lax.rsqrt(jnp.mean(values * values, axis=-1, keepdims=True) + 1e-06) * gain


def local(tokens, modulation, w_qkv, norm_gains, cache_kv, w_out, w_up, w_down):
    own_rows = tokens.shape[0]
    width = HEADS * HEAD_DIM
    scale = 1.0 / math.sqrt(HEAD_DIM)
    residual = tokens.astype(jnp.float32)
    normed = (layer_norm(residual) * (1.0 + modulation[1]) + modulation[0]).astype(jnp.bfloat16)
    qkv_cols = jnp.einsum(
        "td,kda->kta",
        lax.all_gather(normed, "seq", axis=0, tiled=True),
        w_qkv,
        preferred_element_type=jnp.float32,
    ).astype(jnp.bfloat16)
    qkv = lax.all_to_all(qkv_cols, "seq", split_axis=1, concat_axis=2, tiled=True)
    queries = rms_norm(qkv[0].astype(jnp.float32), norm_gains[0]).astype(jnp.bfloat16)
    keys_now = rms_norm(qkv[1].astype(jnp.float32), norm_gains[1]).astype(jnp.bfloat16)
    local_keys = jnp.concatenate([cache_kv[0].reshape(-1, width), keys_now], axis=0)
    local_values = jnp.concatenate([cache_kv[1].reshape(-1, width), qkv[2]], axis=0)
    query_heads = queries.reshape(own_rows, HEADS, HEAD_DIM)
    peak_old = jnp.full((own_rows, HEADS), -1e30, jnp.float32)
    key_piece = lax.all_gather(local_keys, "seq", axis=0, tiled=True)
    value_piece = lax.all_gather(local_values, "seq", axis=0, tiled=True)
    count = key_piece.shape[0]
    scores = (
        jnp.einsum(
            "qhd,khd->qhk",
            query_heads,
            key_piece.reshape(count, HEADS, HEAD_DIM),
            preferred_element_type=jnp.float32,
        )
        * scale
    )
    peak_new = jnp.maximum(peak_old, jnp.max(scores, axis=-1))
    expo = jnp.exp(scores - peak_new[..., None])
    total_new = jnp.sum(expo, axis=-1)
    weights = expo.astype(jnp.bfloat16)
    summed_new = jnp.einsum(
        "qhk,khd->qhd",
        weights,
        value_piece.reshape(count, HEADS, HEAD_DIM),
        preferred_element_type=jnp.float32,
    )
    attended = (summed_new / total_new[..., None]).reshape(own_rows, width).astype(jnp.bfloat16)
    projected_cols = jnp.dot(
        lax.all_gather(attended, "seq", axis=0, tiled=True),
        w_out,
        preferred_element_type=jnp.float32,
    ).astype(jnp.bfloat16)
    projected = lax.all_to_all(projected_cols, "seq", split_axis=0, concat_axis=1, tiled=True)
    residual = residual + modulation[2] * projected.astype(jnp.float32)
    normed2 = (layer_norm(residual) * (1.0 + modulation[4]) + modulation[3]).astype(jnp.bfloat16)
    hidden = jax.nn.gelu(
        jnp.dot(
            lax.all_gather(normed2, "seq", axis=0, tiled=True),
            w_up,
            preferred_element_type=jnp.float32,
        ),
        approximate=True,
    ).astype(jnp.bfloat16)
    feed = lax.psum_scatter(
        jnp.dot(hidden, w_down, preferred_element_type=jnp.float32),
        "seq",
        scatter_dimension=0,
        tiled=True,
    )
    return (residual + modulation[5] * feed).astype(jnp.bfloat16)


def solution(mesh):
    in_specs = (
        P(("groups", "seq"), None),
        P(),
        P(None, None, "seq"),
        P(),
        P(None, None, ("groups", "seq"), None),
        P(None, "seq"),
        P(None, "seq"),
        P("seq", None),
    )
    out_specs = P(("groups", "seq"), None)
    return jax.shard_map(local, mesh=mesh, in_specs=in_specs, out_specs=out_specs, check_vma=False)
```

profile of v0, /device:TPU:0, one launch (start us, length us, event | category | flops | bytes accessed | tf_op | source)
XLA Modules:
  0.0 266.5 jit_solution(11914635441609002521)
XLA Ops:
  6.5 0.0 copy-start
  6.5 1.1 convert_reduce_fusion
  7.6 1.0 fusion.23
  8.6 1.6 fusion.41
  10.2 0.9 fusion.33
  11.1 25.1 %all-gather = bf16[16,3,5120]{2,1,0:T(4,128)(2,1)S(1)} all-gather(bf16[1,3,5120]{2,1,0:T(4,128)(2,1)S(1)} %fusion.33), channel_id=1, replica_groups=mesh['groups'=2,'seq'=16] {'seq'}, dimensions={0}, use_global_device_ids=true | all-gather | bytes 522240 | tf_op jit(solution)/shard_map/all_gather | solution.py:30
  36.2 0.4 reshape.97
  36.7 4.1 %fusion.1 = bf16[3,48,160]{2,1,0:T(8,128)(2,1)S(1)} fusion(bf16[48,5120,1]{1,0,2:T(8,128)(2,1)S(1)} %reshape.97, bf16[3,5120,160]{1,2,0:T(8,128)(2,1)} %param.10), kind=kOutput, calls=%fused_computation.3 | convolution fusion | flops 235952640 | bytes 5452800 | tf_op jit(solution)/shard_map/td,kda->kta/dot_general | solution.py:28
  40.8 0.1 copy.54
  40.8 0.8 reshape.102
  41.6 3.5 %all-to-all-start = ((bf16[16,2,720]{2,1,0:T(2,128)(2,1)}), bf16[16,2,720]{2,1,0:T(2,128)(2,1)S(1)}, u32[]{:S(2)}, u32[]{:S(2)}) async-start(bf16[16,2,720]{2,1,0:T(2,128)(2,1)} %reshape.102), calls=%async_computation | async-start | bytes 98304 | tf_op jit(solution)/shard_map/all_to_all | solution.py:34
  45.1 0.0 all-reduce.3.cloned.1.call-start
  45.1 0.0 copy-done.2
  45.3 0.0 copy-done.3
  45.3 0.1 slice_reduce_fusion
  45.4 6.4 %all-to-all-done = bf16[16,2,720]{2,1,0:T(2,128)(2,1)S(1)} async-done(((bf16[16,2,720]{2,1,0:T(2,128)(2,1)}), bf16[16,2,720]{2,1,0:T(2,128)(2,1)S(1)}, u32[]{:S(2)}, u32[]{:S(2)}) %all-to-all-start) | async-done | bytes 46112 | tf_op jit(solution)/shard_map/all_to_all | solution.py:34
  51.8 0.1 reshape.103
  52.0 0.2 multiply_reduce_fusion.1
  52.3 0.1 reshape.82
  52.4 0.1 squeeze.2
  52.5 0.1 reshape.81
  52.6 0.1 multiply_convert_fusion
  52.7 22.6 %all-gather.2 = bf16[16,9,2560]{2,1,0:T(8,128)(2,1)S(1)} all-gather(bf16[1,9,2560]{2,1,0:T(8,128)(2,1)S(1)} %maximum_bitcast_fusion.1), channel_id=1, replica_groups=mesh['groups'=2,'seq'=16] {'seq'}, dimensions={0}, use_global_device_ids=true | all-gather | bytes 783360 | tf_op jit(solution)/shard_map/all_gather | solution.py:41
  75.4 1.3 reshape.80
  76.7 0.1 multiply_convert_fusion.1
  76.8 1.7 fusion.43
  78.6 22.9 %all-gather.1 = bf16[16,9,2560]{2,1,0:T(8,128)(2,1)S(1)} all-gather(bf16[1,9,2560]{2,1,0:T(8,128)(2,1)S(1)} %maximum_bitcast_fusion), channel_id=1, replica_groups=mesh['groups'=2,'seq'=16] {'seq'}, dimensions={0}, use_global_device_ids=true | all-gather | bytes 783360 | tf_op jit(solution)/shard_map/all_gather | solution.py:42
  101.4 1.3 reshape.79
  102.7 0.2 fusion.29
  102.9 1.5 fusion.4
  104.4 18.9 %all-gather.3 = bf16[16,3,2560]{2,1,0:T(4,128)(2,1)S(1)} all-gather(bf16[1,3,2560]{2,1,0:T(4,128)(2,1)S(1)} %fusion.4), channel_id=1, replica_groups=mesh['groups'=2,'seq'=16] {'seq'}, dimensions={0}, use_global_device_ids=true | all-gather | bytes 261120 | tf_op jit(solution)/shard_map/all_gather | solution.py:65
  123.4 0.2 reshape.91
  123.6 0.0 copy-done
  123.6 0.6 convolution_convert_fusion.1
  124.2 9.3 %all_to_all.28 = bf16[16,3,320]{2,1,0:T(4,128)(2,1)S(1)} all-to-all(bf16[16,3,320]{2,1,0:T(4,128)(2,1)S(1)} %all_to_all.24), channel_id=1, replica_groups=mesh['groups'=2,'seq'=16] {'seq'}, dimensions={0} | all-to-all | bytes 61440 | tf_op jit(solution)/shard_map/all_to_all | solution.py:69
  133.6 0.1 reshape.83
  133.7 0.0 copy-done.1
  133.7 0.2 fusion.40
  133.8 0.2 multiply_reduce_fusion
  134.1 0.1 fusion.32
  134.2 19.5 %all-gather.4 = bf16[16,3,5120]{2,1,0:T(4,128)(2,1)S(1)} all-gather(bf16[1,3,5120]{2,1,0:T(4,128)(2,1)S(1)} %fusion.32), channel_id=1, replica_groups=mesh['groups'=2,'seq'=16] {'seq'}, dimensions={0}, use_global_device_ids=true | all-gather | bytes 522240 | tf_op jit(solution)/shard_map/all_gather | solution.py:74
  153.6 0.4 reshape.93
  154.1 0.0 copy-start.4
  154.1 11.9 %fusion.17 = f32[48,5120]{1,0:T(8,128)} fusion(bf16[864,5120]{1,0:T(8,128)(2,1)} %param.15, bf16[48,5120]{1,0:T(8,128)(2,1)S(1)} %reshape.93, bf16[5120,864]{0,1:T(8,128)(2,1)} %param.14), kind=kOutput, calls=%fused_computation.27 | convolution fusion | flops 849719808 | bytes 19169280 | tf_op jit(solution)/shard_map/dot_general | solution.py:81
  166.0 0.0 all-reduce.3.cloned.1.call-update
  166.1 0.6 dynamic-slice
  167.3 90.7 %all-reduce.3.cloned.1.call-done = f32[48,5120]{1,0:T(8,128)} async-done(((f32[48,5120]{1,0:T(8,128)}), f32[48,5120]{1,0:T(8,128)}) %all-reduce.3.cloned.1.call-update) | async-done | bytes 983056
  258.0 1.6 fusion.28
  (26 shorter events, 0.4 us)
Async XLA Ops:
  6.5 117.0 %copy-start = (bf16[2560,320]{0,1:T(8,128)(2,1)S(1)}, bf16[2560,320]{0,1:T(8,128)(2,1)}, u32[]{:S(2)}) copy-start(bf16[2560,320]{0,1:T(8,128)(2,1)} %param.13) | copy-start | bytes 4915204
  6.5 38.6 %copy-start.2 = (bf16[2,2,3,2560]{3,1,2,0:T(2,128)(2,1)S(1)}, bf16[2,2,3,2560]{3,1,2,0:T(2,128)(2,1)}, u32[]{:S(2)}) copy-start(bf16[2,2,3,2560]{3,1,2,0:T(2,128)(2,1)} %param.12) | copy-start | bytes 184324
  6.5 38.8 %copy-start.3 = (f32[2,2560]{1,0:T(2,128)S(1)}, f32[2,2560]{1,0:T(2,128)}, u32[]{:S(2)}) copy-start(f32[2,2560]{1,0:T(2,128)} %param.11) | copy-start | bytes 61444
  41.6 10.2 %all-to-all-start = ((bf16[16,2,720]{2,1,0:T(2,128)(2,1)}), bf16[16,2,720]{2,1,0:T(2,128)(2,1)S(1)}, u32[]{:S(2)}, u32[]{:S(2)}) async-start(bf16[16,2,720]{2,1,0:T(2,128)(2,1)} %reshape.102), calls=%async_computation | async-start | bytes 98304 | tf_op jit(solution)/shard_map/all_to_all | solution.py:34
  45.1 212.9 %all-reduce.3.cloned.1.call-start = ((), (), s32[]{:S(2)}) async-start(), calls=%async_computation.2 | async-start | bytes 1966080
  76.8 56.9 %copy-start.1 = (bf16[3,5120]{1,0:T(4,128)(2,1)S(1)}, bf16[3,5120]{1,0:T(4,128)(2,1)}, u32[]{:S(2)}) copy-start(bf16[3,5120]{1,0:T(4,128)(2,1)} %param.8) | copy-start | bytes 92164
  154.1 12.0 %copy-start.4 = (u32[32]{0:T(128)S(1)}, u32[32]{0:T(128)}, u32[]{:S(2)}) copy-start(u32[32]{0:T(128)} %constant.33) | copy-start | bytes 388
Sparse Core Ops, SparseCore 0:
  166.2 91.7 all-reduce.2
where the time goes:
time: 267 us; the launch traced here: 266 us
  blocking collectives  118 us (44%)
  waiting for transfers between devices  97.1 us (36%)
  matrix products  19.9 us (7%)
  between operations  14.3 us (5%)
  other arithmetic  7.35 us (3%)
  local copies, waits for them, and re-layouts  5.94 us (2%)
  starting transfers between devices  3.54 us (1%)
    unnamed x2, waiting for transfers between devices  90.7 us
    all_gather x1, blocking collectives, local(): lax.all_gather(normed, 'seq', axis=0, tiled=True)  25.1 us
    all_gather x1, blocking collectives, local(): value_piece = lax.all_gather(local_values, 'seq', axis=0, tiled=True)  22.9 us
    all_gather x1, blocking collectives, local(): key_piece = lax.all_gather(local_keys, 'seq', axis=0, tiled=True)  22.6 us
    all_gather x1, blocking collectives, local(): lax.all_gather(normed2, 'seq', axis=0, tiled=True)  19.5 us
    all_gather x1, blocking collectives, local(): lax.all_gather(attended, 'seq', axis=0, tiled=True)  18.9 us
    dot_general x1, matrix products, local(): jnp.dot(hidden, w_down, preferred_element_type=jnp.float32)  11.9 us
    all_to_all x1, blocking collectives, local(): lax.all_to_all(projected_cols, 'seq', split_axis=0, concat_axis=1, tiled=...  9.34 us
  transfers between devices with their start and end apart: 2, of which 2 were waited for; matrix products, arithmetic and copies ran while one was open for 0% of the time, Pallas kernels for 0%

commit v1 on v0

v1 whole, which is shorter than its diff:
```python
import math

import jax
import jax.numpy as jnp
from jax import lax
from jax.experimental import pallas as pl
from jax.experimental.pallas import tpu as pltpu
from jax.sharding import PartitionSpec as P

HEAD_DIM = 128
HEADS = 20
MESH = pl.DeviceIdType.MESH


def layer_norm(values):
    center = values - jnp.mean(values, axis=-1, keepdims=True)
    spread = jnp.mean(center * center, axis=-1, keepdims=True)
    return center * lax.rsqrt(spread + 1e-06)


def exchange(cid, n, gs, items):
    kinds = [kind for kind, _ in items]
    arrays = [array for _, array in items]
    count = len(items)
    outs = []
    for kind, array in items:
        block = array.shape if kind in ("all", "peer") else array.shape[1:]
        outs.append(jax.ShapeDtypeStruct(((gs if kind == "peer" else n),) + block, array.dtype))

    def body(*refs):
        ins, dsts = refs[:count], refs[count : 2 * count]
        send, recv, own = refs[2 * count :]
        me = lax.axis_index("seq")
        base = me - me % gs

        def source(k, j):
            if kinds[k] == "each":
                return ins[k].at[j]
            if kinds[k] == "block":
                return ins[k].at[j // gs]
            return ins[k]

        def other(k, i):
            if kinds[k] == "peer":
                return base + (me + i) % gs
            return (me + i) % n

        def row(k, j):
            return j % gs if kinds[k] == "peer" else j

        def steps(k):
            return gs if kinds[k] == "peer" else n

        barrier = pltpu.get_barrier_semaphore()

        def greet(i, c):
            pl.semaphore_signal(barrier, inc=1, device_id={"seq": (me + i) % n}, device_id_type=MESH)
            return c

        lax.fori_loop(1, n, greet, 0)
        locals_ = []
        for k in range(count):
            copy = pltpu.make_async_copy(source(k, me), dsts[k].at[row(k, me)], own.at[k])
            copy.start()
            locals_.append(copy)
        pl.semaphore_wait(barrier, n - 1)

        def remote(k, j, mark):
            return pltpu.make_async_remote_copy(
                src_ref=source(k, j),
                dst_ref=dsts[k].at[row(k, mark)],
                send_sem=send.at[k, j],
                recv_sem=recv.at[k, mark],
                device_id={"seq": j},
                device_id_type=MESH,
            )

        for k in range(count):
            def launch(i, c, k=k):
                remote(k, other(k, i), me).start()
                return c

            lax.fori_loop(1, steps(k), launch, 0)
        for copy in locals_:
            copy.wait()
        for k in range(count):
            def finish(i, c, k=k):
                j = other(k, i)
                copy = remote(k, j, j)
                copy.wait_recv()
                copy.wait_send()
                return c

            lax.fori_loop(1, steps(k), finish, 0)

    return pl.pallas_call(
        body,
        out_shape=outs,
        in_specs=[pl.BlockSpec(memory_space=pl.ANY)] * count,
        out_specs=[pl.BlockSpec(memory_space=pl.ANY)] * count,
        scratch_shapes=[
            pltpu.SemaphoreType.DMA((count, n)),
            pltpu.SemaphoreType.DMA((count, n)),
            pltpu.SemaphoreType.DMA((count,)),
        ],
        compiler_params=pltpu.CompilerParams(collective_id=cid, has_side_effects=True),
    )(*arrays)


def local(n, tokens, modulation, w_qkv, norm_gains, cache_kv, w_out, w_up, w_down):
    own_rows, features = tokens.shape
    width = HEADS * HEAD_DIM
    cols = w_qkv.shape[2]
    wide = math.lcm(cols, HEAD_DIM)
    gs = wide // cols
    blocks = n // gs
    heads = wide // HEAD_DIM
    frames = cache_kv.shape[1]
    total_rows = n * own_rows
    query_rows = total_rows // gs
    scale = 1.0 / math.sqrt(HEAD_DIM)
    me = lax.axis_index("seq")
    block, place = me // gs, me % gs

    (all_tokens,) = exchange(0, n, gs, [("all", tokens)])
    all_tokens = all_tokens.reshape(total_rows, features).astype(jnp.float32)
    normed = (layer_norm(all_tokens) * (1.0 + modulation[1]) + modulation[0]).astype(jnp.bfloat16)
    qkv_cols = [
        jnp.dot(normed, w_qkv[i], preferred_element_type=jnp.float32).astype(jnp.bfloat16) for i in range(3)
    ]
    squares = jnp.stack([jnp.sum(jnp.square(qkv_cols[i].astype(jnp.float32)), axis=-1) for i in range(2)])
    cache_blocks = cache_kv.reshape(2 * frames * own_rows, blocks, wide).transpose(1, 0, 2)
    cached, pieces, squares = exchange(
        1, n, gs, [("block", cache_blocks), ("peer", jnp.stack(qkv_cols)), ("all", squares)]
    )
    inverse = lax.rsqrt(jnp.sum(squares, axis=0) / width + 1e-06)
    pieces = pieces.transpose(1, 2, 0, 3).reshape(3, total_rows, wide)
    gains = lax.dynamic_slice_in_dim(norm_gains, block * wide, wide, axis=1)
    first = place * query_rows
    queries = (
        lax.dynamic_slice_in_dim(pieces[0], first, query_rows, axis=0).astype(jnp.float32)
        * lax.dynamic_slice_in_dim(inverse[0], first, query_rows, axis=0)[:, None]
        * gains[0]
    ).astype(jnp.bfloat16)
    keys_now = (pieces[1].astype(jnp.float32) * inverse[1][:, None] * gains[1]).astype(jnp.bfloat16)
    cached = cached.reshape(n, 2, frames * own_rows, wide).transpose(1, 0, 2, 3).reshape(2, -1, wide)
    keys = jnp.concatenate([cached[0], keys_now], axis=0).reshape(-1, heads, HEAD_DIM)
    values = jnp.concatenate([cached[1], pieces[2]], axis=0).reshape(-1, heads, HEAD_DIM)
    queries = queries.reshape(query_rows, heads, HEAD_DIM)
    scores = jnp.einsum("qhd,khd->hqk", queries, keys, preferred_element_type=jnp.float32) * scale
    expo = jnp.exp(scores - jnp.max(scores, axis=-1, keepdims=True))
    total = jnp.sum(expo, axis=-1, keepdims=True)
    summed = jnp.einsum("hqk,khd->hqd", expo.astype(jnp.bfloat16), values, preferred_element_type=jnp.float32)
    attended = (summed / total).astype(jnp.bfloat16).transpose(1, 0, 2).reshape(query_rows, wide)

    (attended,) = exchange(2, n, gs, [("all", attended)])
    attended = attended.reshape(blocks, total_rows, wide).transpose(1, 0, 2).reshape(total_rows, width)
    projected_cols = jnp.dot(attended, w_out, preferred_element_type=jnp.float32).astype(jnp.bfloat16)
    (projected,) = exchange(3, n, gs, [("all", projected_cols)])
    projected = projected.transpose(1, 0, 2).reshape(total_rows, features)
    residual = all_tokens + modulation[2] * projected.astype(jnp.float32)
    normed2 = (layer_norm(residual) * (1.0 + modulation[4]) + modulation[3]).astype(jnp.bfloat16)
    hidden = jax.nn.gelu(
        jnp.dot(normed2, w_up, preferred_element_type=jnp.float32), approximate=True
    ).astype(jnp.bfloat16)
    partial = jnp.dot(hidden, w_down, preferred_element_type=jnp.float32).astype(jnp.bfloat16)
    (partial,) = exchange(4, n, gs, [("each", partial.reshape(n, own_rows, features))])
    feed = jnp.sum(partial.astype(jnp.float32), axis=0)
    own = lax.dynamic_slice_in_dim(residual, me * own_rows, own_rows, axis=0)
    return (own + modulation[5] * feed).astype(jnp.bfloat16)


def solution(mesh):
    n = mesh.shape["seq"]
    in_specs = (
        P(("groups", "seq"), None),
        P(),
        P(None, None, "seq"),
        P(),
        P(None, None, ("groups", "seq"), None),
        P(None, "seq"),
        P(None, "seq"),
        P("seq", None),
    )
    out_specs = P(("groups", "seq"), None)

    def step(*args):
        return local(n, *args)

    return jax.shard_map(step, mesh=mesh, in_specs=in_specs, out_specs=out_specs, check_vma=False)
```

time: 267 us -> 132 us (0.49)
  the two profiles are of different devices: /device:TPU:0 before, /device:TPU:15 now
where the time goes in v1:
time: 132 us; the launch traced here: 131 us
  Pallas kernels  82.8 us (63%)
  matrix products  19.1 us (14%)
  other arithmetic  15.3 us (12%)
  local copies, waits for them, and re-layouts  13.7 us (10%)
    pallas_call x5, Pallas kernels, exchange(): pl.pallas_call(body, out_shape=outs, in_specs=[pl.BlockSpec(memory_space=...  82.8 us
    dot_general x1, matrix products, local(): jnp.dot(hidden, w_down, preferred_element_type=jnp.float32)  11 us
    dot_general x3, matrix products, local(): jnp.dot(normed, w_qkv[i], preferred_element_type=jnp.float32)  6.44 us
    convert_element_type x3, local copies, waits for them, and re-layouts, local(): residual = all_tokens + modulation[2] * projected.astype(jnp.float32)  3.6 us
    reduce_sum x2, other arithmetic, layer_norm(): center = values - jnp.mean(values, axis=-1, keepdims=True)  3.43 us

profile of v1, /device:TPU:15, one launch (start us, length us, event | category | flops | bytes accessed | tf_op | source)
XLA Modules:
  0.0 131.3 jit_solution(8104173580849800701)
XLA Ops:
  0.0 20.2 %shard_map.82 = bf16[16,3,5120]{2,1,0:T(4,128)(2,1)} custom-call(bf16[3,5120]{1,0:T(4,128)(2,1)} %refs_0_.1), custom_call_target="tpu_custom_call" | custom-call | tf_op jit(solution)/shard_map/pallas_call | solution.py:96
  20.2 1.5 %convert_reduce_fusion.1 = f32[16,3]{1,0:T(8,128)S(1)} fusion(bf16[16,3,5120]{2,1,0:T(4,128)(2,1)} %shard_map.82), kind=kLoop, calls=%fused_computation.16 | loop fusion | flops 491472 | bytes 491712 | tf_op jit(solution)/shard_map/reduce_sum | solution.py:16
  21.7 1.7 %multiply_reduce_fusion.1 = f32[16,3]{1,0:T(8,128)S(1)} fusion(bf16[16,3,5120]{2,1,0:T(4,128)(2,1)} %shard_map.82, f32[16,3]{1,0:T(8,128)S(1)} %broadcast_multiply_fusion.1), kind=kLoop, calls=%fused_computation.14 | loop fusion | flops 982992 | bytes 491904 | tf_op jit(solution)/shard_map/reduce_sum | solution.py:17
  23.4 0.1 fusion.63
  23.5 0.6 add_convert_fusion
  24.1 0.4 convert_element_type.101
  24.5 2.2 %multiply_reduce_fusion.3 = (f32[48]{0:T(128)S(1)}, bf16[48,160]{1,0:T(8,128)(2,1)S(1)}) fusion(bf16[48,5120]{1,0:T(8,128)(2,1)S(1)} %convert_element_type.101, bf16[3,5120,160]{1,2,0:T(8,128)(2,1)} %param.10), kind=kOutput, calls=%fused_computation.64 | convolution fusion | flops 78673872 | bytes 2145472 | tf_op jit(solution)/shard_map/dot_general | solution.py:129
  26.7 2.2 %multiply_reduce_fusion.2 = (f32[48]{0:T(128)S(1)}, bf16[48,160]{1,0:T(8,128)(2,1)S(1)}) fusion(bf16[48,5120]{1,0:T(8,128)(2,1)S(1)} %convert_element_type.101, bf16[3,5120,160]{1,2,0:T(8,128)(2,1)} %param.10), kind=kOutput, calls=%fused_computation.63 | convolution fusion | flops 78673872 | bytes 2145472 | tf_op jit(solution)/shard_map/dot_general | solution.py:129
  28.9 2.1 %fusion.20 = bf16[1,48,160]{2,1,0:T(8,128)(2,1)S(1)} fusion(bf16[48,5120]{1,0:T(8,128)(2,1)S(1)} %convert_element_type.101, bf16[3,5120,160]{1,2,0:T(8,128)(2,1)} %param.10), kind=kOutput, calls=%fused_computation.25 | convolution fusion | flops 78650880 | bytes 2145280 | tf_op jit(solution)/shard_map/dot_general | solution.py:129
  31.0 0.6 pad_maximum_fusion.refs_1_
  31.6 0.6 pad_maximum_fusion.1.refs_2_
  32.3 0.6 copy.39
  32.9 13.1 %shard_map.83 = (bf16[16,12,640]{2,1,0:T(8,128)(2,1)}, bf16[4,3,48,160]{3,2,1,0:T(8,128)(2,1)}, f32[16,2,48]{2,1,0:T(2,128)}) custom-call(bf16[4,12,640]{2,1,0:T(8,128)(2,1)} %bitcast.73, bf16[3,48,160]{2,1,0:T(8,128)(2,1)} %pad_maximum_fusion.refs_1_, f32[2,48]{1,0:T(2,128)} %pad_maximum_fusion.1.refs_2_), custom_call_target="tpu_custom_call" | custom-call | tf_op jit(solution)/shard_map/pallas_call | solution.py:96
  46.0 1.1 fusion.61
  47.2 0.1 squeeze.22
  47.3 0.7 reduce_sum.85
  48.1 0.9 dynamic-slice_reduce_fusion.1
  49.0 0.1 multiply_convert_fusion
  49.1 0.1 copy.15
  49.3 0.2 reshape.207
  49.4 0.1 fusion.44
  49.6 0.2 concatenate.14
  49.8 0.3 fusion.65
  50.1 0.2 fusion.49
  50.4 0.2 concatenate.16
  50.6 0.1 concatenate.17
  50.8 0.2 fusion.19
  51.0 0.6 copy.28
  51.7 12.5 %shard_map.84 = bf16[16,12,640]{2,1,0:T(8,128)(2,1)} custom-call(bf16[12,640]{1,0:T(8,128)(2,1)} %bitcast.79), custom_call_target="tpu_custom_call" | custom-call | tf_op jit(solution)/shard_map/pallas_call | solution.py:96
  64.2 1.0 reshape.203
  65.2 1.2 convolution_convert_fusion.1.refs_0_
  66.5 18.1 %shard_map.85 = bf16[16,48,320]{2,1,0:T(8,128)(2,1)} custom-call(bf16[48,320]{1,0:T(8,128)(2,1)} %convolution_convert_fusion.1.refs_0_), custom_call_target="tpu_custom_call" | custom-call | tf_op jit(solution)/shard_map/pallas_call | solution.py:96
  84.5 1.1 convert_bitcast_fusion
  85.7 0.4 copy.25
  86.1 1.9 %reshape.209 = f32[16,3,5120]{2,1,0:T(4,128)} reshape(f32[48,16,320]{2,1,0:T(8,128)S(1)} %copy.25) | data formatting | bytes 1966080 | tf_op jit(solution)/shard_map/convert_element_type | solution.py:161
  88.0 1.9 %fusion.23 = f32[16,3]{1,0:T(8,128)S(1)} fusion(f32[16,3,5120]{2,1,0:T(4,128)} %reshape.209, bf16[16,3,5120]{2,1,0:T(4,128)(2,1)S(1)} %copy-done.1, f32[5120]{0:T(1024)S(1)} %bitcast.70), kind=kLoop, calls=%fused_computation.28 | loop fusion | flops 982992 | bytes 1495232 | tf_op jit(solution)/shard_map/reduce_sum | solution.py:16
  89.9 0.7 multiply_reduce_fusion
  90.6 0.6 add_rsqrt_fusion
  91.2 1.3 %rsqrt.25 = f32[48]{0:T(128)} reshape(f32[16,3]{1,0:T(8,128)} %add_rsqrt_fusion) | data formatting | bytes 384 | tf_op jit(solution)/shard_map/rsqrt | solution.py:18
  92.6 1.3 div.50
  93.9 1.3 %reshape.208 = f32[48,5120]{1,0:T(8,128)} reshape(f32[48,16,320]{2,1,0:T(8,128)S(1)} %copy.25) | data formatting | bytes 1966080 | tf_op jit(solution)/shard_map/convert_element_type | solution.py:161
  95.2 1.3 %reshape.206 = f32[48,5120]{1,0:T(8,128)} reshape(bf16[16,3,5120]{2,1,0:T(4,128)(2,1)S(1)} %copy-done.1) | data formatting | bytes 1474560 | tf_op jit(solution)/shard_map/convert_element_type | solution.py:126
  96.5 1.6 %multiply_add_fusion.1 = f32[48,5120]{1,0:T(8,128)S(1)} fusion(f32[48,5120]{1,0:T(8,128)} %reshape.206, f32[48,5120]{1,0:T(8,128)} %reshape.208, f32[5120]{0:T(1024)S(1)} %bitcast.72), kind=kLoop, calls=%fused_computation.27 | loop fusion | flops 491520 | bytes 2969600 | tf_op jit(solution)/shard_map/add | solution.py:161
  98.2 11.0 %convolution_convert_fusion = bf16[48,5120]{1,0:T(8,128)(2,1)S(1)} fusion(bf16[864,5120]{1,0:T(8,128)(2,1)} %param.15, bf16[5120,864]{0,1:T(8,128)(2,1)} %param.14, f32[48,5120]{1,0:T(8,128)S(1)} %multiply_add_fusion.1, f32[5120]{0:T(1024)S(1)} %bitcast.76, f32[5120]{0:T(1024)S(1)} %bitcast.77, f32[48]{0:T(128)S(1)} %copy-done.7, f32[48]{0:T(128)S(1)} %copy-done.8), kind=kOutput, calls=%fused_computation | convolution fusion | flops 851194368 | bytes 19210624 | tf_op jit(solution)/shard_map/dot_general | solution.py:166
  109.1 1.1 reshape.205.refs_0_
  110.3 19.0 %shard_map.86 = bf16[16,3,5120]{2,1,0:T(4,128)(2,1)} custom-call(bf16[16,3,5120]{2,1,0:T(4,128)(2,1)} %reshape.205.refs_0_), custom_call_target="tpu_custom_call" | custom-call | tf_op jit(solution)/shard_map/pallas_call | solution.py:96
  129.2 1.4 %convert_reduce_fusion = f32[3,5120]{1,0:T(4,128)S(1)} fusion(bf16[16,3,5120]{2,1,0:T(4,128)(2,1)} %shard_map.86), kind=kLoop, calls=%fused_computation.10 | loop fusion | flops 476160 | bytes 552960 | tf_op jit(solution)/shard_map/reduce_sum | solution.py:168
  130.6 0.7 add_convert_fusion.9
  (39 shorter events, 0.6 us)
Async XLA Ops:
  0.0 65.2 %copy-start = (bf16[2560,320]{0,1:T(8,128)(2,1)S(1)}, bf16[2560,320]{0,1:T(8,128)(2,1)}, u32[]{:S(2)}) copy-start(bf16[2560,320]{0,1:T(8,128)(2,1)} %param.13) | copy-start | bytes 4915204
  0.0 23.4 %copy-start.4 = (f32[6,5120]{1,0:T(8,128)S(1)}, f32[6,5120]{1,0:T(8,128)}, u32[]{:S(2)}) copy-start(f32[6,5120]{1,0:T(8,128)} %param.9) | copy-start | bytes 368644
  20.2 3.3 %copy-start.1 = (bf16[16,3,5120]{2,1,0:T(4,128)(2,1)S(1)}, bf16[16,3,5120]{2,1,0:T(4,128)(2,1)}, u32[]{:S(2)}) copy-start(bf16[16,3,5120]{2,1,0:T(4,128)(2,1)} %shard_map.82) | copy-start | bytes 1474564
  28.9 3.3 %copy-start.6 = (bf16[2,2,3,2560]{3,1,2,0:T(2,128)(2,1)S(1)}, bf16[2,2,3,2560]{3,1,2,0:T(2,128)(2,1)}, u32[]{:S(2)}) copy-start(bf16[2,2,3,2560]{3,1,2,0:T(2,128)(2,1)} %param.12) | copy-start | bytes 184324
  46.0 3.5 %copy-start.3 = (bf16[16,12,640]{2,1,0:T(8,128)(2,1)S(1)}, bf16[16,12,640]{2,1,0:T(8,128)(2,1)}, u32[]{:S(2)}) copy-start(bf16[16,12,640]{2,1,0:T(8,128)(2,1)} %get-tuple-element.10) | copy-start | bytes 737284
  88.0 1.9 %copy-start.2 = (f32[16,3,5120]{2,1,0:T(4,128)S(1)}, f32[16,3,5120]{2,1,0:T(4,128)}, u32[]{:S(2)}) copy-start(f32[16,3,5120]{2,1,0:T(4,128)} %reshape.209) | copy-start | bytes 2949124
  89.9 0.7 copy-start.5
  96.5 1.6 %copy-start.7 = (f32[48]{0:T(128)S(1)}, f32[48]{0:T(128)}, u32[]{:S(2)}) copy-start(f32[48]{0:T(128)} %rsqrt.25) | copy-start | bytes 580
  96.5 1.6 %copy-start.8 = (f32[48]{0:T(128)S(1)}, f32[48]{0:T(128)}, u32[]{:S(2)}) copy-start(f32[48]{0:T(128)} %div.50) | copy-start | bytes 580

commit v2 on v1

--- a/solution.py
+++ b/solution.py
@@ -18,13 +18,46 @@
     return center * lax.rsqrt(spread + 1e-06)
 
 
+def factors(n):
+    chips = n // 2
+    near = 1
+    while (2 * near) * (2 * near) <= chips:
+        near *= 2
+    return chips // near, near
+
+
+def remote_copy(src, dst, send, recv, device):
+    return pltpu.make_async_remote_copy(
+        src_ref=src, dst_ref=dst, send_sem=send, recv_sem=recv, device_id={"seq": device}, device_id_type=MESH
+    )
+
+
+def loop(low, high, fn):
+    def step(i, c):
+        fn(i)
+        return c
+
+    lax.fori_loop(low, high, step, 0)
+
+
+def greet(n, me):
+    barrier = pltpu.get_barrier_semaphore()
+
+    def signal(i):
+        pl.semaphore_signal(barrier, inc=1, device_id={"seq": (me + i) % n}, device_id_type=MESH)
+
+    loop(1, n, signal)
+    return barrier
+
+
 def exchange(cid, n, gs, items):
     kinds = [kind for kind, _ in items]
     arrays = [array for _, array in items]
     count = len(items)
+    far, near = factors(n)
     outs = []
     for kind, array in items:
-        block = array.shape if kind in ("all", "peer") else array.shape[1:]
+        block = array.shape[1:] if kind == "block" else array.shape
         outs.append(jax.ShapeDtypeStruct(((gs if kind == "peer" else n),) + block, array.dtype))
 
     def body(*refs):
@@ -32,66 +65,92 @@
         send, recv, own = refs[2 * count :]
         me = lax.axis_index("seq")
         base = me - me % gs
-
-        def source(k, j):
-            if kinds[k] == "each":
-                return ins[k].at[j]
-            if kinds[k] == "block":
-                return ins[k].at[j // gs]
-            return ins[k]
-
-        def other(k, i):
-            if kinds[k] == "peer":
-                return base + (me + i) % gs
-            return (me + i) % n
-
-        def row(k, j):
-            return j % gs if kinds[k] == "peer" else j
-
-        def steps(k):
-            return gs if kinds[k] == "peer" else n
-
-        barrier = pltpu.get_barrier_semaphore()
-
-        def greet(i, c):
-            pl.semaphore_signal(barrier, inc=1, device_id={"seq": (me + i) % n}, device_id_type=MESH)
-            return c
-
-        lax.fori_loop(1, n, greet, 0)
+        a, b, c = me // (2 * near), (me // 2) % near, me % 2
+        barrier = greet(n, me)
+
+        def dev(a2, b2, c2):
+            return (a2 * near + b2) * 2 + c2
+
+        def first(k, a2):
+            return ins[k].at[(a2 * 2 * near) // gs] if kinds[k] == "block" else ins[k]
+
+        def far_copy(k, i, mark):
+            a2 = (a + i) % far
+            return remote_copy(first(k, a2), dsts[k].at[mark], send.at[k, 0, i], recv.at[k, mark], dev(a2, b, c))
+
+        def near_copy(k, i, j):
+            row = dev((a + far - i) % far, b, c)
+            src = first(k, a) if isinstance(i, int) else dsts[k].at[row]
+            return remote_copy(
+                src, dsts[k].at[row], send.at[k, 1, i * near + j], recv.at[k, row], dev(a, (b + j) % near, c)
+            )
+
+        def core_copy(k, i, j):
+            row = dev((a + far - i) % far, (b + near - j) % near, c)
+            src = first(k, a) if isinstance(i, int) else dsts[k].at[row]
+            return remote_copy(src, dsts[k].at[row], send.at[k, 2, i * near + j], recv.at[k, row], dev(a, b, 1 - c))
+
+        def arrived(k, row):
+            remote_copy(dsts[k].at[row], dsts[k].at[row], send.at[k, 0, 0], recv.at[k, row], me).wait_recv()
+
+        def peer_copy(k, i, mark):
+            return remote_copy(
+                ins[k], dsts[k].at[mark], send.at[k, 0, i], recv.at[k, mark], base + (me + i) % gs
+            )
+
+        tree = [k for k in range(count) if kinds[k] != "peer"]
+        direct = [k for k in range(count) if kinds[k] == "peer"]
         locals_ = []
         for k in range(count):
-            copy = pltpu.make_async_copy(source(k, me), dsts[k].at[row(k, me)], own.at[k])
+            if k in tree:
+                copy = pltpu.make_async_copy(first(k, a), dsts[k].at[me], own.at[k])
+            else:
+                copy = pltpu.make_async_copy(ins[k], dsts[k].at[me % gs], own.at[k])
             copy.start()
             locals_.append(copy)
         pl.semaphore_wait(barrier, n - 1)
-
-        def remote(k, j, mark):
-            return pltpu.make_async_remote_copy(
-                src_ref=source(k, j),
-                dst_ref=dsts[k].at[row(k, mark)],
-                send_sem=send.at[k, j],
-                recv_sem=recv.at[k, mark],
-                device_id={"seq": j},
-                device_id_type=MESH,
-            )
-
-        for k in range(count):
-            def launch(i, c, k=k):
-                remote(k, other(k, i), me).start()
-                return c
-
-            lax.fori_loop(1, steps(k), launch, 0)
+        for k in tree:
+            loop(1, far, lambda i: far_copy(k, i, me).start())
+        for k in direct:
+            loop(1, gs, lambda i: peer_copy(k, i, me % gs).start())
+        for k in tree:
+            loop(1, near, lambda j: near_copy(k, 0, j).start())
+            core_copy(k, 0, 0).start()
+        for k in tree:
+
+            def forward(i):
+                arrived(k, dev((a + far - i) % far, b, c))
+                loop(1, near, lambda j: near_copy(k, i, j).start())
+                core_copy(k, i, 0 * i).start()
+
+            loop(1, far, forward)
+        for k in tree:
+
+            def across(m):
+                j, i = 1 + m // far, m % far
+                arrived(k, dev((a + far - i) % far, (b + near - j) % near, c))
+                core_copy(k, i, j).start()
+
+            loop(0, far * (near - 1), across)
         for copy in locals_:
             copy.wait()
-        for k in range(count):
-            def finish(i, c, k=k):
-                j = other(k, i)
-                copy = remote(k, j, j)
-                copy.wait_recv()
-                copy.wait_send()
-                return c
-
-            lax.fori_loop(1, steps(k), finish, 0)
+        for k in direct:
+
+            def finish(i):
+                peer_copy(k, i, (me + i) % gs).wait_recv()
+                peer_copy(k, i, me % gs).wait_send()
+
+            loop(1, gs, finish)
+        for k in tree:
+            loop(0, n // 2, lambda m: arrived(k, 2 * m + 1 - c))
+            loop(1, far, lambda i: far_copy(k, i, me).wait_send())
+
+            def drain(m):
+                i, j = m // near, m % near
+                core_copy(k, i, j).wait_send()
+
+            loop(0, far * near, drain)
+            loop(0, far * (near - 1), lambda m: near_copy(k, m % far, 1 + m // far).wait_send())
 
     return pl.pallas_call(
         body,
@@ -99,12 +158,109 @@
         in_specs=[pl.BlockSpec(memory_space=pl.ANY)] * count,
         out_specs=[pl.BlockSpec(memory_space=pl.ANY)] * count,
         scratch_shapes=[
-            pltpu.SemaphoreType.DMA((count, n)),
+            pltpu.SemaphoreType.DMA((count, 3, max(far * near, gs))),
             pltpu.SemaphoreType.DMA((count, n)),
             pltpu.SemaphoreType.DMA((count,)),
         ],
         compiler_params=pltpu.CompilerParams(collective_id=cid, has_side_effects=True),
     )(*arrays)
+
+
+def reduce_exchange(cid, n, parts):
+    far, near = factors(n)
+    _, rows, features = parts.shape
+    block = (rows, features)
+
+    def body(x, out, got1, sum1, got2, sum2, got3, send, recv1, recv2, recv3):
+        me = lax.axis_index("seq")
+        a, b, c = me // (2 * near), (me // 2) % near, me % 2
+        barrier = greet(n, me)
+
+        def dev(a2, b2, c2):
+            return (a2 * near + b2) * 2 + c2
+
+        def spot(m):
+            j, i = m // far, m % far
+            return (a + 1 + i) % far, (b + 1 + j) % near
+
+        def copy1(m):
+            a2, b2 = spot(m)
+            at = a2 * near + b2
+            return remote_copy(x.at[dev(a2, b2, 1 - c)], got1.at[at], send.at[0, at], recv1.at[at], dev(a, b, 1 - c))
+
+        def copy2(m, mark):
+            a2, b2 = spot(m)
+            at = a2 * near + b2
+            return remote_copy(
+                sum1.at[at], got2.at[a2 * near + mark], send.at[1, at], recv2.at[a2 * near + mark], dev(a, b2, c)
+            )
+
+        def copy3(i, mark):
+            a2 = (a + i) % far
+            return remote_copy(sum2.at[a2], got3.at[mark], send.at[2, a2], recv3.at[mark], dev(a2, b, c))
+
+        def wide(v):
+            return v.astype(jnp.float32)
+
+        pl.semaphore_wait(barrier, n - 1)
+        loop(0, far * near, lambda m: copy1(m).start())
+
+        def pair(m):
+            a2, b2 = spot(m)
+            at = a2 * near + b2
+            remote_copy(got1.at[at], got1.at[at], send.at[0, at], recv1.at[at], dev(a, b, 1 - c)).wait_recv()
+            return wide(x[dev(a2, b2, c)]) + wide(got1[at])
+
+        def hand(m):
+            a2, b2 = spot(m)
+            sum1[a2 * near + b2] = pair(m).astype(sum1.dtype)
+            copy2(m, b).start()
+
+        loop(0, far * (near - 1), hand)
+
+        def collect(i):
+            a2 = (a + i) % far
+            total = pair(far * (near - 1) + i - 1)
+            for j in range(1, near):
+                at = a2 * near + (b + j) % near
+                remote_copy(got2.at[at], got2.at[at], send.at[1, at], recv2.at[at], dev(a, b, 1 - c)).wait_recv()
+                total = total + wide(got2[at])
+            return a2, total
+
+        def ship(i):
+            a2, total = collect(i)
+            sum2[a2] = total.astype(sum2.dtype)
+            copy3(i, a).start()
+
+        loop(1, far, ship)
+        _, total = collect(far)
+        for i in range(1, far):
+            copy3(i, (a + i) % far).wait_recv()
+            total = total + wide(got3[(a + i) % far])
+        out[...] = total
+        loop(0, far * near, lambda m: copy1(m).wait_send())
+        loop(0, far * (near - 1), lambda m: copy2(m, b).wait_send())
+        loop(1, far, lambda i: copy3(i, a).wait_send())
+
+    dtype = parts.dtype
+    return pl.pallas_call(
+        body,
+        out_shape=jax.ShapeDtypeStruct(block, jnp.float32),
+        in_specs=[pl.BlockSpec(memory_space=pltpu.VMEM)],
+        out_specs=pl.BlockSpec(memory_space=pltpu.VMEM),
+        scratch_shapes=[
+            pltpu.VMEM((far * near,) + block, dtype),
+            pltpu.VMEM((far * near,) + block, dtype),
+            pltpu.VMEM((far * near,) + block, dtype),
+            pltpu.VMEM((far,) + block, dtype),
+            pltpu.VMEM((far,) + block, dtype),
+            pltpu.SemaphoreType.DMA((3, far * near)),
+            pltpu.SemaphoreType.DMA((far * near,)),
+            pltpu.SemaphoreType.DMA((far * near,)),
+            pltpu.SemaphoreType.DMA((far,)),
+        ],
+        compiler_params=pltpu.CompilerParams(collective_id=cid, has_side_effects=True),
+    )(parts)
 
 
 def local(n, tokens, modulation, w_qkv, norm_gains, cache_kv, w_out, w_up, w_down):
@@ -164,8 +320,7 @@
         jnp.dot(normed2, w_up, preferred_element_type=jnp.float32), approximate=True
     ).astype(jnp.bfloat16)
     partial = jnp.dot(hidden, w_down, preferred_element_type=jnp.float32).astype(jnp.bfloat16)
-    (partial,) = exchange(4, n, gs, [("each", partial.reshape(n, own_rows, features))])
-    feed = jnp.sum(partial.astype(jnp.float32), axis=0)
+    feed = reduce_exchange(4, n, partial.reshape(n, own_rows, features))
     own = lax.dynamic_slice_in_dim(residual, me * own_rows, own_rows, axis=0)
     return (own + modulation[5] * feed).astype(jnp.bfloat16)
 

time: 132 us -> 117 us (0.89)
  the two profiles are of different devices: /device:TPU:15 before, /device:TPU:0 now
where the time goes in v2:
time: 117 us; the launch traced here: 116 us
  Pallas kernels  68.1 us (58%)
  matrix products  19.1 us (16%)
  other arithmetic  14.8 us (13%)
  local copies, waits for them, and re-layouts  13.7 us (12%)
    pallas_call x4, Pallas kernels, exchange(): pl.pallas_call(body, out_shape=outs, in_specs=[pl.BlockSpec(memory_space=...  53.5 us
    pallas_call x1, Pallas kernels, reduce_exchange(): pl.pallas_call(body, out_shape=jax.ShapeDtypeStruct(block, jnp.float32),...  14.7 us
    dot_general x1, matrix products, local(): jnp.dot(hidden, w_down, preferred_element_type=jnp.float32)  11 us
    dot_general x3, matrix products, local(): jnp.dot(normed, w_qkv[i], preferred_element_type=jnp.float32)  6.45 us
    convert_element_type x3, local copies, waits for them, and re-layouts, local(): residual = all_tokens + modulation[2] * projected.astype(jnp.float32)  3.6 us
    reduce_sum x2, other arithmetic, layer_norm(): center = values - jnp.mean(values, axis=-1, keepdims=True)  3.43 us
    reduce_sum x2, other arithmetic, layer_norm(): spread = jnp.mean(center * center, axis=-1, keepdims=True)  2.39 us

profile of v2, /device:TPU:0, one launch (start us, length us, event | category | flops | bytes accessed | tf_op | source)
XLA Modules:
  0.0 116.1 jit_solution(1107934971336935773)
XLA Ops:
  0.0 15.6 %shard_map.82 = bf16[16,3,5120]{2,1,0:T(4,128)(2,1)} custom-call(bf16[3,5120]{1,0:T(4,128)(2,1)} %refs_0_.1), custom_call_target="tpu_custom_call" | custom-call | tf_op jit(solution)/shard_map/pallas_call | solution.py:155
  15.6 1.5 %convert_reduce_fusion = f32[16,3]{1,0:T(8,128)S(1)} fusion(bf16[16,3,5120]{2,1,0:T(4,128)(2,1)} %shard_map.82), kind=kLoop, calls=%fused_computation.15 | loop fusion | flops 491472 | bytes 491712 | tf_op jit(solution)/shard_map/reduce_sum | solution.py:16
  17.1 1.7 %multiply_reduce_fusion.1 = f32[16,3]{1,0:T(8,128)S(1)} fusion(bf16[16,3,5120]{2,1,0:T(4,128)(2,1)} %shard_map.82, f32[16,3]{1,0:T(8,128)S(1)} %broadcast_multiply_fusion.1), kind=kLoop, calls=%fused_computation.13 | loop fusion | flops 982992 | bytes 491904 | tf_op jit(solution)/shard_map/reduce_sum | solution.py:17
  18.8 0.1 fusion.63
  18.9 0.6 add_convert_fusion
  19.5 0.4 convert_element_type.98
  19.9 2.2 %multiply_reduce_fusion.3 = (f32[48]{0:T(128)S(1)}, bf16[48,160]{1,0:T(8,128)(2,1)S(1)}) fusion(bf16[48,5120]{1,0:T(8,128)(2,1)S(1)} %convert_element_type.98, bf16[3,5120,160]{1,2,0:T(8,128)(2,1)} %param.10), kind=kOutput, calls=%fused_computation.63 | convolution fusion | flops 78673872 | bytes 2145472 | tf_op jit(solution)/shard_map/dot_general | solution.py:285
  22.1 2.2 %multiply_reduce_fusion.2 = (f32[48]{0:T(128)S(1)}, bf16[48,160]{1,0:T(8,128)(2,1)S(1)}) fusion(bf16[48,5120]{1,0:T(8,128)(2,1)S(1)} %convert_element_type.98, bf16[3,5120,160]{1,2,0:T(8,128)(2,1)} %param.10), kind=kOutput, calls=%fused_computation.62 | convolution fusion | flops 78673872 | bytes 2145472 | tf_op jit(solution)/shard_map/dot_general | solution.py:285
  24.3 2.1 %fusion.20 = bf16[1,48,160]{2,1,0:T(8,128)(2,1)S(1)} fusion(bf16[48,5120]{1,0:T(8,128)(2,1)S(1)} %convert_element_type.98, bf16[3,5120,160]{1,2,0:T(8,128)(2,1)} %param.10), kind=kOutput, calls=%fused_computation.24 | convolution fusion | flops 78650880 | bytes 2145280 | tf_op jit(solution)/shard_map/dot_general | solution.py:285
  26.4 0.6 pad_maximum_fusion.refs_1_
  27.1 0.6 pad_maximum_fusion.1.refs_2_
  27.7 0.6 copy.40
  28.4 13.5 %shard_map.83 = (bf16[16,12,640]{2,1,0:T(8,128)(2,1)}, bf16[4,3,48,160]{3,2,1,0:T(8,128)(2,1)}, f32[16,2,48]{2,1,0:T(2,128)}) custom-call(bf16[4,12,640]{2,1,0:T(8,128)(2,1)} %bitcast.73, bf16[3,48,160]{2,1,0:T(8,128)(2,1)} %pad_maximum_fusion.refs_1_, f32[2,48]{1,0:T(2,128)} %pad_maximum_fusion.1.refs_2_), custom_call_target="tpu_custom_call" | custom-call | tf_op jit(solution)/shard_map/pallas_call | solution.py:155
  41.9 1.1 fusion.61
  43.0 0.1 squeeze.22
  43.1 0.7 reduce_sum.76
  43.9 0.1 fusion.54
  44.0 0.9 dynamic-slice_reduce_fusion.1
  44.9 0.1 multiply_convert_fusion
  45.0 0.1 copy.16
  45.1 0.2 reshape.207
  45.3 0.1 fusion.44
  45.5 0.2 concatenate.14
  45.7 0.3 fusion.65
  46.0 0.2 fusion.49
  46.2 0.2 concatenate.16
  46.5 0.1 concatenate.17
  46.6 0.2 fusion.19
  46.9 0.6 copy.29
  47.5 11.7 %shard_map.84 = bf16[16,12,640]{2,1,0:T(8,128)(2,1)} custom-call(bf16[12,640]{1,0:T(8,128)(2,1)} %bitcast.79), custom_call_target="tpu_custom_call" | custom-call | tf_op jit(solution)/shard_map/pallas_call | solution.py:155
  59.2 1.0 reshape.203
  60.2 1.2 %convolution_convert_fusion.1.refs_0_ = bf16[48,320]{1,0:T(8,128)(2,1)} fusion(bf16[48,2560]{1,0:T(8,128)(2,1)S(1)} %bitcast.69, bf16[2560,320]{0,1:T(8,128)(2,1)S(1)} %copy-done), kind=kOutput, calls=%fused_computation.17 | convolution fusion | flops 78658560 | bytes 1914880 | tf_op jit(solution)/shard_map/dot_general | solution.py:314
  61.5 12.7 %shard_map.85 = bf16[16,48,320]{2,1,0:T(8,128)(2,1)} custom-call(bf16[48,320]{1,0:T(8,128)(2,1)} %convolution_convert_fusion.1.refs_0_), custom_call_target="tpu_custom_call" | custom-call | tf_op jit(solution)/shard_map/pallas_call | solution.py:155
  74.2 1.1 convert_bitcast_fusion
  75.3 0.4 copy.26
  75.7 1.9 %reshape.209 = f32[16,3,5120]{2,1,0:T(4,128)} reshape(f32[48,16,320]{2,1,0:T(8,128)S(1)} %copy.26) | data formatting | bytes 1966080 | tf_op jit(solution)/shard_map/convert_element_type | solution.py:317
  77.6 1.9 %fusion.23 = f32[16,3]{1,0:T(8,128)S(1)} fusion(f32[16,3,5120]{2,1,0:T(4,128)} %reshape.209, bf16[16,3,5120]{2,1,0:T(4,128)(2,1)S(1)} %copy-done.1, f32[5120]{0:T(1024)S(1)} %bitcast.70), kind=kLoop, calls=%fused_computation.27 | loop fusion | flops 982992 | bytes 1495232 | tf_op jit(solution)/shard_map/reduce_sum | solution.py:16
  79.5 0.7 multiply_reduce_fusion
  80.3 0.6 add_rsqrt_fusion
  80.9 1.3 %rsqrt.25 = f32[48]{0:T(128)} reshape(f32[16,3]{1,0:T(8,128)} %add_rsqrt_fusion) | data formatting | bytes 384 | tf_op jit(solution)/shard_map/rsqrt | solution.py:18
  82.2 1.3 %div.50 = f32[48]{0:T(128)} reshape(f32[16,3]{1,0:T(8,128)} %copy-done.5) | data formatting | bytes 384 | tf_op jit(solution)/shard_map/div | solution.py:16
  83.5 1.3 %reshape.208 = f32[48,5120]{1,0:T(8,128)} reshape(f32[48,16,320]{2,1,0:T(8,128)S(1)} %copy.26) | data formatting | bytes 1966080 | tf_op jit(solution)/shard_map/convert_element_type | solution.py:317
  84.8 1.3 %reshape.206 = f32[48,5120]{1,0:T(8,128)} reshape(bf16[16,3,5120]{2,1,0:T(4,128)(2,1)S(1)} %copy-done.1) | data formatting | bytes 1474560 | tf_op jit(solution)/shard_map/convert_element_type | solution.py:282
  86.1 1.6 %multiply_add_fusion.1 = f32[48,5120]{1,0:T(8,128)S(1)} fusion(f32[48,5120]{1,0:T(8,128)} %reshape.206, f32[48,5120]{1,0:T(8,128)} %reshape.208, f32[5120]{0:T(1024)S(1)} %bitcast.72), kind=kLoop, calls=%fused_computation.26 | loop fusion | flops 491520 | bytes 2969600 | tf_op jit(solution)/shard_map/add | solution.py:317
  87.8 11.0 %convolution_convert_fusion = bf16[48,5120]{1,0:T(8,128)(2,1)S(1)} fusion(bf16[864,5120]{1,0:T(8,128)(2,1)} %param.15, bf16[5120,864]{0,1:T(8,128)(2,1)} %param.14, f32[48,5120]{1,0:T(8,128)S(1)} %multiply_add_fusion.1, f32[5120]{0:T(1024)S(1)} %bitcast.76, f32[5120]{0:T(1024)S(1)} %bitcast.77, f32[48]{0:T(128)S(1)} %copy-done.7, f32[48]{0:T(128)S(1)} %copy-done.8), kind=kOutput, calls=%fused_computation | convolution fusion | flops 851194368 | bytes 19210624 | tf_op jit(solution)/shard_map/dot_general | solution.py:322
  98.7 1.1 reshape.205.x
  99.9 14.7 %shard_map.86 = f32[3,5120]{1,0:T(4,128)} custom-call(bf16[16,3,5120]{2,1,0:T(4,128)(2,1)} %reshape.205.x), custom_call_target="tpu_custom_call" | custom-call | tf_op jit(solution)/shard_map/pallas_call | solution.py:246
  114.6 1.6 %add_convert_fusion.9 = bf16[3,5120]{1,0:T(4,128)(2,1)} fusion(f32[3,5120]{1,0:T(4,128)} %shard_map.86, f32[48,5120]{1,0:T(8,128)S(1)} %multiply_add_fusion.1, s32[]{:T(128)S(6)} %select_n.25, f32[5120]{0:T(1024)S(1)} %bitcast.78), kind=kLoop, calls=%fused_computation.57 | loop fusion | flops 46080 | bytes 174084 | tf_op jit(solution)/shard_map/convert_element_type | solution.py:325
  (38 shorter events, 0.6 us)
Async XLA Ops:
  0.0 60.2 %copy-start = (bf16[2560,320]{0,1:T(8,128)(2,1)S(1)}, bf16[2560,320]{0,1:T(8,128)(2,1)}, u32[]{:S(2)}) copy-start(bf16[2560,320]{0,1:T(8,128)(2,1)} %param.13) | copy-start | bytes 4915204
  0.0 18.8 %copy-start.4 = (f32[6,5120]{1,0:T(8,128)S(1)}, f32[6,5120]{1,0:T(8,128)}, u32[]{:S(2)}) copy-start(f32[6,5120]{1,0:T(8,128)} %param.9) | copy-start | bytes 368644
  15.6 3.3 %copy-start.1 = (bf16[16,3,5120]{2,1,0:T(4,128)(2,1)S(1)}, bf16[16,3,5120]{2,1,0:T(4,128)(2,1)}, u32[]{:S(2)}) copy-start(bf16[16,3,5120]{2,1,0:T(4,128)(2,1)} %shard_map.82) | copy-start | bytes 1474564
  24.3 3.3 %copy-start.6 = (bf16[2,2,3,2560]{3,1,2,0:T(2,128)(2,1)S(1)}, bf16[2,2,3,2560]{3,1,2,0:T(2,128)(2,1)}, u32[]{:S(2)}) copy-start(bf16[2,2,3,2560]{3,1,2,0:T(2,128)(2,1)} %param.12) | copy-start | bytes 184324
  41.9 3.5 %copy-start.3 = (bf16[16,12,640]{2,1,0:T(8,128)(2,1)S(1)}, bf16[16,12,640]{2,1,0:T(8,128)(2,1)}, u32[]{:S(2)}) copy-start(bf16[16,12,640]{2,1,0:T(8,128)(2,1)} %get-tuple-element.10) | copy-start | bytes 737284
  77.6 1.9 %copy-start.2 = (f32[16,3,5120]{2,1,0:T(4,128)S(1)}, f32[16,3,5120]{2,1,0:T(4,128)}, u32[]{:S(2)}) copy-start(f32[16,3,5120]{2,1,0:T(4,128)} %reshape.209) | copy-start | bytes 2949124
  79.5 0.7 copy-start.5
  86.1 1.6 %copy-start.7 = (f32[48]{0:T(128)S(1)}, f32[48]{0:T(128)}, u32[]{:S(2)}) copy-start(f32[48]{0:T(128)} %rsqrt.25) | copy-start | bytes 580
  86.1 1.6 %copy-start.8 = (f32[48]{0:T(128)S(1)}, f32[48]{0:T(128)}, u32[]{:S(2)}) copy-start(f32[48]{0:T(128)} %div.50) | copy-start | bytes 580
